TPU v7x, 32 devices: a whole 2x2x4 slice. The times are simulated.
32 devices in a mesh: seq: 8 (over z, x), dp: 4 (over y, core).
Axes of the slice: x: 2, y: 2, z: 4, core: 2. Of those that a mesh axis runs over, the one named last changes fastest.
Arguments:
- inputs: bfloat16 [4, 1024, 8192], P('dp', 'seq'), may hold values from -8 to 8
- adapter_down_weight: bfloat16 [8192, 128], replicated, may hold values from -0.0625 to 0.0625
- adapter_up_weight: bfloat16 [384, 128], replicated, may hold values from -0.3125 to 0.3125
- query: bfloat16 [4, 1024, 128], P('dp', 'seq'), may hold values from -6 to 6
- key: bfloat16 [4, 1024, 128], P('dp', 'seq'), may hold values from -6 to 6
- value: bfloat16 [4, 1024, 128], P('dp', 'seq'), may hold values from -6 to 6
- output_gradient: bfloat16 [4, 1024, 128], P('dp', 'seq'), may hold values from -6 to 6
Outputs:
- query_grad: bfloat16 [4, 1024, 128], P('dp', 'seq')
- key_grad: bfloat16 [4, 1024, 128], P('dp', 'seq')
- value_grad: bfloat16 [4, 1024, 128], P('dp', 'seq')
- down_grad: float32 [8192, 128], P('dp')
- up_grad: float32 [384, 128], P('dp')
All inputs are finite; a program needn't handle non-finite values.
Results may differ from a plain program's by a relative error of at most 0.0058.
Values sent between devices are 32-bit elements; how exact they have to be, the bound alone decides.
A program may use at most 64 MiB of HBM per device.

v0:
```python
import math

import jax
import jax.numpy as jnp
from jax import lax
from jax.sharding import PartitionSpec as P

HEAD_SIZE = 128
LOCAL_HEADS = 1


def entering(part, axis, combine, identity, reverse):
    count = lax.axis_size(axis)
    place = lax.axis_index(axis)
    ahead = count - 1 - place if reverse else place
    gathered = lax.all_gather(part, axis)
    state = jnp.zeros_like(part) + jnp.asarray(identity, part.dtype)

    def one(turn, state):
        source = count - 1 - turn if reverse else turn
        return combine(state, lax.dynamic_index_in_dim(gathered, source, 0, False))

    return lax.fori_loop(0, ahead, one, state)


def add_states(earlier, later):
    return earlier + later


def rounded_values(array):
    return array.astype(jnp.bfloat16)


def local(inputs, adapter_down_weight, adapter_up_weight, query, key, value, output_gradient):
    rows = query.shape[1]
    width = query.shape[2]
    seq_count = lax.axis_size("seq")
    dp_count = lax.axis_size("dp")
    length = rows * seq_count
    factor = 1.0 / math.sqrt(HEAD_SIZE * length)
    queries = query.reshape(rows, LOCAL_HEADS, HEAD_SIZE)
    keys = key.reshape(rows, LOCAL_HEADS, HEAD_SIZE)
    values = value.reshape(rows, LOCAL_HEADS, HEAD_SIZE)
    grads_out = output_gradient.reshape(rows, LOCAL_HEADS, HEAD_SIZE)
    kv_state = jnp.einsum("thi,thj->hij", keys, values, preferred_element_type=jnp.float32)
    qg_state = jnp.einsum("thi,thj->hij", queries, grads_out, preferred_element_type=jnp.float32)
    zeros = jnp.zeros_like(kv_state)
    prefix = entering(kv_state, "seq", add_states, zeros, False)
    suffix = entering(qg_state, "seq", add_states, zeros, True)
    prefix = rounded_values(prefix)
    suffix = rounded_values(suffix)
    rows_idx = lax.broadcasted_iota(jnp.int32, (rows, rows), 0)
    cols_idx = lax.broadcasted_iota(jnp.int32, (rows, rows), 1)
    causal = rows_idx >= cols_idx
    grad_scores = rounded_values(
        jnp.where(
            causal,
            jnp.einsum("thj,shj->hts", grads_out, values, preferred_element_type=jnp.float32),
            0.0,
        )
    )
    scores = rounded_values(
        jnp.where(
            causal,
            jnp.einsum("thi,shi->hts", queries, keys, preferred_element_type=jnp.float32),
            0.0,
        )
    )
    query_grad = jnp.einsum(
        "hts,shi->thi", grad_scores, keys, preferred_element_type=jnp.float32
    ) + jnp.einsum("thj,hij->thi", grads_out, prefix, preferred_element_type=jnp.float32)
    key_grad = jnp.einsum(
        "hts,thi->shi", grad_scores, queries, preferred_element_type=jnp.float32
    ) + jnp.einsum("shj,hij->shi", values, suffix, preferred_element_type=jnp.float32)
    value_grad = jnp.einsum(
        "hts,thj->shj", scores, grads_out, preferred_element_type=jnp.float32
    ) + jnp.einsum("shi,hij->shj", keys, suffix, preferred_element_type=jnp.float32)
    query_grad = rounded_values(factor * query_grad).reshape(rows, width)
    key_grad = rounded_values(factor * key_grad).reshape(rows, width)
    value_grad = rounded_values(factor * value_grad).reshape(rows, width)
    flattened = inputs.reshape(rows, inputs.shape[2])
    gradient_list = jnp.concatenate([query_grad, key_grad, value_grad], axis=1)
    low_rank_state = rounded_values(
        jnp.dot(flattened, adapter_down_weight, preferred_element_type=jnp.float32)
    )
    low_rank_gradient = rounded_values(
        jnp.dot(gradient_list, adapter_up_weight, preferred_element_type=jnp.float32)
    )
    inverse = 1.0 / math.sqrt(length * dp_count)
    contract = (((0,), (0,)), ((), ()))
    down_part = lax.psum_scatter(
        lax.dot_general(flattened, low_rank_gradient, contract, preferred_element_type=jnp.float32)
        * inverse,
        "dp",
        scatter_dimension=0,
        tiled=True,
    )
    up_term = (
        lax.dot_general(gradient_list, low_rank_state, contract, preferred_element_type=jnp.float32)
        * inverse
    )
    up_part = lax.psum_scatter(up_term, "dp", scatter_dimension=0, tiled=True)
    down_grad, up_grad = lax.psum((down_part, up_part), "seq")
    return (
        query_grad.reshape(1, rows, width),
        key_grad.reshape(1, rows, width),
        value_grad.reshape(1, rows, width),
        down_grad,
        up_grad,
    )


def solution(mesh):
    return jax.shard_map(
        local,
        mesh=mesh,
        in_specs=(
            P("dp", "seq", None),
            P(),
            P(),
            P("dp", "seq", None),
            P("dp", "seq", None),
            P("dp", "seq", None),
            P("dp", "seq", None),
        ),
        out_specs=(
            P("dp", "seq", None),
            P("dp", "seq", None),
            P("dp", "seq", None),
            P("dp", None),
            P("dp", None),
        ),
        check_vma=False,
    )
```

profile of v0, /device:TPU:0, one launch (start us, length us, event | category | flops | bytes accessed | tf_op | source)
XLA Modules:
  0.0 241.8 jit_solution(8446664571541854131)
XLA Ops:
  7.2 1.1 fusion.21
  8.3 0.9 fusion.7
  9.3 1.0 convolution_bitcast_fusion.1
  10.2 1.0 fusion.28
  11.2 1.0 convolution_bitcast_fusion.2
  12.3 1.1 convolution_bitcast_fusion
  13.4 33.2 %all-gather.1 = f32[1024,128]{1,0:T(8,128)S(1)} all-gather(f32[128,128]{1,0:T(8,128)S(1)} %fusion.21), channel_id=3, replica_groups=mesh['seq'=8,'dp'=4] {'seq'}, dimensions={0}, use_global_device_ids=true | all-gather | bytes 589824 | tf_op jit(solution)/shard_map/all_gather | solution.py:16
  46.6 0.3 while.23
  46.9 31.2 %all-gather = f32[1024,128]{1,0:T(8,128)S(1)} all-gather(f32[128,128]{1,0:T(8,128)S(1)} %fusion.28), channel_id=2, replica_groups=mesh['seq'=8,'dp'=4] {'seq'}, dimensions={0}, use_global_device_ids=true | all-gather | bytes 589824 | tf_op jit(solution)/shard_map/all_gather | solution.py:16
  78.1 0.2 fusion.9
  78.3 0.2 fusion.11
  78.5 0.2 fusion.8
  78.6 2.9 %fusion = f32[8192,128]{0,1:T(8,128)} fusion(bf16[1,128,8192]{2,1,0:T(8,128)(2,1)S(1)} %copy-done, bf16[384,128]{1,0:T(8,128)(2,1)S(1)} %copy-done.4, bf16[128,128]{0,1:T(8,128)(2,1)S(1)} %bitcast.100, bf16[128,128]{0,1:T(8,128)(2,1)S(1)} %bitcast.103, bf16[128,128]{0,1:T(8,128)(2,1)S(1)} %bitcast.106), kind=kOutput, calls=%fused_computation.3 | convolution fusion | flops 282378240 | bytes 6488064 | tf_op jit(solution)/shard_map/dot_general | solution.py:92
  81.5 0.0 reduce-scatter.5.cloned.1.call-start
  81.6 3.1 %convolution_multiply_fusion.1 = f32[384,128]{1,0:T(8,128)} fusion(bf16[8192,128]{1,0:T(8,128)(2,1)} %param.12, bf16[1,128,8192]{2,1,0:T(8,128)(2,1)S(1)} %copy-done, bf16[128,128]{0,1:T(8,128)(2,1)S(1)} %bitcast.101, bf16[128,128]{0,1:T(8,128)(2,1)S(1)} %bitcast.104, bf16[128,128]{0,1:T(8,128)(2,1)S(1)} %bitcast.107), kind=kOutput, calls=%fused_computation.7 | convolution fusion | flops 281378816 | bytes 4489216 | tf_op jit(solution)/shard_map/dot_general | solution.py:99
  84.7 0.0 all-reduce.2.cloned.1.call-start
  84.8 43.0 %reduce-scatter.3.cloned.1.call-done = f32[2048,128]{0,1:T(8,128)} async-done(((f32[8192,128]{0,1:T(8,128)}), f32[2048,128]{0,1:T(8,128)}) %reduce-scatter.3.cloned.1.call-update) | async-done | bytes 1048592 | tf_op jit(solution)/shard_map/reduce_scatter | solution.py:91
  127.8 0.7 copy.15
  128.5 0.7 copy.14
  129.2 0.7 copy.16
  129.9 20.6 %reduce-scatter.5.cloned.1.call-done = f32[96,128]{1,0:T(8,128)} async-done(((f32[384,128]{1,0:T(8,128)}), f32[96,128]{1,0:T(8,128)}) %reduce-scatter.5.cloned.1.call-update) | async-done | bytes 49168 | tf_op jit(solution)/shard_map/reduce_scatter | solution.py:102
  150.6 39.1 %psum.15 = f32[96,128]{1,0:T(8,128)} all-reduce(f32[96,128]{1,0:T(8,128)} %reduce-scatter.5.cloned.1.call-done), channel_id=1, replica_groups=mesh['seq'=8,'dp'=4] {'seq'}, use_global_device_ids=true, to_apply=%region_7.8 | all-reduce | flops 12288 | bytes 98304 | tf_op jit(solution)/shard_map/psum | solution.py:103
  189.7 43.0 %all-reduce.2.cloned.1.call-done = f32[2048,128]{0,1:T(8,128)} async-done(((f32[2048,128]{0,1:T(8,128)}), f32[2048,128]{0,1:T(8,128)}) %all-reduce.2.cloned.1.call-update) | async-done | bytes 1048592 | tf_op jit(solution)/shard_map/psum | solution.py:103
  232.7 2.5 %copy.17 = f32[2048,128]{1,0:T(8,128)} copy(f32[2048,128]{0,1:T(8,128)} %all-reduce.2.cloned.1.call-done) | data formatting | bytes 2097152
  (24 shorter events, 0.2 us)
Async XLA Ops:
  7.2 71.5 %copy-start = (bf16[1,128,8192]{2,1,0:T(8,128)(2,1)S(1)}, bf16[1,128,8192]{2,1,0:T(8,128)(2,1)}, u32[]{:S(2)}) copy-start(bf16[1,128,8192]{2,1,0:T(8,128)(2,1)} %param.11) | copy-start | bytes 6291460
  7.2 120.6 %reduce-scatter.3.cloned.1.call-start = ((), (), s32[]{:S(2)}) async-start(), calls=%async_computation.2 | async-start | bytes 5242880 | tf_op jit(solution)/shard_map/reduce_scatter | solution.py:91
  9.3 68.8 %copy-start.3 = (bf16[1,128,128]{2,1,0:T(8,128)(2,1)S(1)}, bf16[1,128,128]{2,1,0:T(8,128)(2,1)}, u32[]{:S(2)}) copy-start(bf16[1,128,128]{2,1,0:T(8,128)(2,1)} %param.16) | copy-start | bytes 98308
  11.2 67.0 %copy-start.2 = (bf16[1,128,128]{2,1,0:T(8,128)(2,1)S(1)}, bf16[1,128,128]{2,1,0:T(8,128)(2,1)}, u32[]{:S(2)}) copy-start(bf16[1,128,128]{2,1,0:T(8,128)(2,1)} %param.15) | copy-start | bytes 98308
  12.2 66.2 %copy-start.1 = (bf16[1,128,128]{2,1,0:T(8,128)(2,1)S(1)}, bf16[1,128,128]{2,1,0:T(8,128)(2,1)}, u32[]{:S(2)}) copy-start(bf16[1,128,128]{2,1,0:T(8,128)(2,1)} %param.17) | copy-start | bytes 98308
  13.4 65.2 %copy-start.4 = (bf16[384,128]{1,0:T(8,128)(2,1)S(1)}, bf16[384,128]{1,0:T(8,128)(2,1)}, u32[]{:S(2)}) copy-start(bf16[384,128]{1,0:T(8,128)(2,1)} %param.13) | copy-start | bytes 294916
  81.5 69.0 %reduce-scatter.5.cloned.1.call-start = ((), (), s32[]{:S(2)}) async-start(), calls=%async_computation.4 | async-start | bytes 245760 | tf_op jit(solution)/shard_map/reduce_scatter | solution.py:102
  84.7 148.0 %all-reduce.2.cloned.1.call-start = ((), (), s32[]{:S(2)}) async-start(), calls=%async_computation.3 | async-start | bytes 2097152 | tf_op jit(solution)/shard_map/psum | solution.py:103
Sparse Core Ops, SparseCore 0:
  81.7 46.0 reduce-scatter.2
  130.8 19.7 reduce-scatter.4
  154.1 78.5 all-reduce.1
where the time goes:
time: 242 us
  waiting for transfers between devices  107 us (44%)
  blocking collectives  104 us (43%)
  between operations  13.9 us (6%)
  matrix products  12.6 us (5%)
  local copies, waits for them, and re-layouts  4.74 us (2%)
    all_gather x2, blocking collectives, entering(): gathered = lax.all_gather(part, axis)  64.4 us
    psum x1, waiting for transfers between devices, local(): down_grad, up_grad = lax.psum((down_part, up_part), 'seq')  43 us
    reduce_scatter x1, waiting for transfers between devices, local(): lax.psum_scatter(lax.dot_general(flattened, low_rank_gradient, contract,...  43 us
    psum x1, blocking collectives, local(): down_grad, up_grad = lax.psum((down_part, up_part), 'seq')  39.1 us
    reduce_scatter x1, waiting for transfers between devices, local(): up_part = lax.psum_scatter(up_term, 'dp', scatter_dimension=0, tiled=True)  20.6 us
  transfers between devices with their start and end apart: 3, of which 3 were waited for; matrix products, arithmetic and copies ran while one was open for 2% of the time, Pallas kernels for 0%

commit v1 on v0

--- a/solution.py
+++ b/solution.py
@@ -1,8 +1,11 @@
+import functools
 import math
 
 import jax
 import jax.numpy as jnp
 from jax import lax
+from jax.experimental import pallas as pl
+from jax.experimental.pallas import tpu as pltpu
 from jax.sharding import PartitionSpec as P
 
 HEAD_SIZE = 128
@@ -110,9 +113,306 @@
     )
 
 
+MESH = pl.DeviceIdType.MESH
+CORES = 2
+CHUNKS = 8
+
+
+def fits(seq_count, dp_count):
+    depth = seq_count // 2
+    return dp_count == 2 * CORES and depth >= 2 and seq_count % 2 == 0 and depth & (depth - 1) == 0
+
+
+def dot(a, b, da, db):
+    return lax.dot_general(a, b, (((da,), (db,)), ((), ())), preferred_element_type=jnp.float32)
+
+
+def fused_kernel(
+    depth, factor, inverse,
+    x_hbm, w_hbm, u_ref, q_ref, k_ref, v_ref, g_ref,
+    qo_ref, ko_ref, vo_ref, down_ref, up_ref,
+    x_ref, w_ref, xs_ref, xr_ref, xt_ref,
+    st_ref, kvr_ref, qgr_ref, sxs_ref, sxr_ref,
+    ls_ref, lr_ref, ups_ref, upr_ref, fg_ref,
+    ys_ref, yr_ref, acc_ref, xrs_ref, zs_ref, zr_ref,
+    load_sem, core_s, core_r, kv_s, kv_r, qg_s, qg_r, sx_s, sx_r,
+    y_s, y_r, x_s, x_r, z_s, z_r, a_s, a_r,
+):
+    seq = lax.axis_index("seq")
+    dp = lax.axis_index("dp")
+    z, x = seq // 2, seq % 2
+    y, c = dp // CORES, dp % CORES
+    mate = {"seq": seq, "dp": y * CORES + (1 - c)}
+    across = {"seq": seq, "dp": (1 - y) * CORES + c}
+    beside = {"seq": z * 2 + (1 - x), "dp": dp}
+
+    def along(other):
+        return {"seq": other * 2 + x, "dp": dp}
+
+    load_x = pltpu.make_async_copy(x_hbm, x_ref, load_sem.at[0])
+    load_w = pltpu.make_async_copy(w_hbm, w_ref, load_sem.at[1])
+    load_x.start()
+    load_w.start()
+
+    barrier = pltpu.get_barrier_semaphore()
+    friends = [mate, across, beside] + [along(lax.rem(z + d, depth)) for d in range(1, depth)]
+    for friend in friends:
+        pl.semaphore_signal(barrier, inc=1, device_id=friend, device_id_type=MESH)
+
+    rows = q_ref.shape[0]
+    shard = down_ref.shape[0]
+    ushard = up_ref.shape[0]
+    width = q_ref.shape[1]
+    q, k, v, g = q_ref[...], k_ref[...], v_ref[...], g_ref[...]
+    st_ref[0] = dot(k, v, 0, 0)
+    st_ref[1] = dot(q, g, 0, 0)
+    pl.semaphore_wait(barrier, len(friends))
+
+    def remote(src, dst, ssem, rsem, where):
+        return pltpu.make_async_remote_copy(
+            src_ref=src, dst_ref=dst, send_sem=ssem, recv_sem=rsem, device_id=where, device_id_type=MESH
+        )
+
+    ups, downs = [], []
+    for d in range(1, depth):
+        ups.append(remote(st_ref.at[0], kvr_ref.at[d - 1], kv_s.at[d - 1], kv_r.at[d - 1], along(lax.rem(z + d, depth))))
+        downs.append(remote(st_ref.at[1], qgr_ref.at[d - 1], qg_s.at[d - 1], qg_r.at[d - 1], along(lax.rem(z - d + depth, depth))))
+    for d in range(1, depth):
+        pl.when(z + d < depth)(ups[d - 1].start)
+        pl.when(z >= d)(downs[d - 1].start)
+
+    load_x.wait()
+    core_copies = []
+    for part in range(2):
+        cols = pl.ds(pl.multiple_of((part * CORES + 1 - c) * shard, 128), shard)
+        xs_ref[part] = x_ref[:, cols].astype(jnp.float32)
+        copy = remote(xs_ref.at[part], xr_ref.at[part], core_s.at[part], core_r.at[part], mate)
+        copy.start()
+        core_copies.append(copy)
+
+    r_idx = lax.broadcasted_iota(jnp.int32, (rows, rows), 0)
+    c_idx = lax.broadcasted_iota(jnp.int32, (rows, rows), 1)
+    causal = r_idx >= c_idx
+    gs = jnp.where(causal, dot(g, v, 1, 1), 0.0).astype(jnp.bfloat16)
+    sc = jnp.where(causal, dot(q, k, 1, 1), 0.0).astype(jnp.bfloat16)
+    q_in = dot(gs, k, 1, 0)
+    k_in = dot(gs, q, 0, 0)
+    v_in = dot(sc, g, 0, 0)
+
+    for part in range(2):
+        cols = pl.ds(pl.multiple_of((part * CORES + c) * shard, 128), shard)
+        xt_ref[part, :, 0:rows] = x_ref[:, cols].T
+
+    sxs_ref[...] = jnp.zeros_like(sxs_ref)
+    for d in range(1, depth):
+        @pl.when(z >= d)
+        def _(d=d):
+            ups[d - 1].wait_recv()
+            sxs_ref[0] += kvr_ref[d - 1]
+
+        @pl.when(z + d < depth)
+        def _(d=d):
+            downs[d - 1].wait_recv()
+            sxs_ref[1] += qgr_ref[d - 1]
+
+    prefix = sxs_ref[0]
+    suffix = sxs_ref[1]
+
+    @pl.when(x == 0)
+    def _():
+        sxs_ref[0] += st_ref[0]
+
+    @pl.when(x == 1)
+    def _():
+        sxs_ref[1] += st_ref[1]
+
+    swap = remote(sxs_ref, sxr_ref, sx_s, sx_r, beside)
+    swap.start()
+
+    load_w.wait()
+    low = jnp.dot(x_ref[...], w_ref[...], preferred_element_type=jnp.float32).astype(jnp.bfloat16)
+    for part in range(2):
+        core_copies[part].wait_recv()
+        xt_ref[part, :, rows:] = xr_ref[part].astype(jnp.bfloat16).T
+
+    swap.wait_recv()
+    prefix = (prefix + sxr_ref[0]).astype(jnp.bfloat16)
+    suffix = (suffix + sxr_ref[1]).astype(jnp.bfloat16)
+    q_grad = (factor * (q_in + dot(g, prefix, 1, 1))).astype(jnp.bfloat16)
+    k_grad = (factor * (k_in + dot(v, suffix, 1, 1))).astype(jnp.bfloat16)
+    v_grad = (factor * (v_in + dot(k, suffix, 1, 0))).astype(jnp.bfloat16)
+    fg = jnp.concatenate([q_grad, k_grad, v_grad], axis=1)
+    low_grad = dot(fg, u_ref[...], 1, 0).astype(jnp.bfloat16)
+    ls_ref[...] = low_grad.astype(jnp.float32)
+    low_copy = remote(ls_ref, lr_ref, core_s.at[2], core_r.at[2], mate)
+    low_copy.start()
+    qo_ref[...] = q_grad
+    ko_ref[...] = k_grad
+    vo_ref[...] = v_grad
+
+    up_all = dot(fg, low, 0, 0)
+    fg_ref[...] = up_all
+    for part in range(2):
+        rng = pl.ds(pl.multiple_of((part * CORES + 1 - c) * ushard, 8), ushard)
+        ups_ref[part] = fg_ref[rng, :]
+    up_copy = remote(ups_ref, upr_ref, core_s.at[3], core_r.at[3], mate)
+    up_copy.start()
+
+    low_copy.wait_recv()
+    both = jnp.concatenate([low_grad, lr_ref[...].astype(jnp.bfloat16)], axis=0)
+
+    size = shard // CHUNKS
+    pieces = [(i * size, size) for i in range(CHUNKS)] + [(shard, ushard)]
+    count = len(pieces)
+
+    def partial(i, part):
+        off, n = pieces[i]
+        if off < shard:
+            return jnp.dot(xt_ref[part, off : off + n, :], both, preferred_element_type=jnp.float32)
+        mine = pl.ds(pl.multiple_of((part * CORES + c) * ushard, 8), ushard)
+        return fg_ref[mine, :] + upr_ref[part]
+
+    def half(i, which):
+        off, n = pieces[i]
+        return pl.ds(pl.multiple_of(off + which * (n // 2), 8), n // 2)
+
+    def place(i, which):
+        off, n = pieces[i]
+        if off < shard:
+            return down_ref.at[half(i, which), :]
+        return up_ref.at[pl.ds(pl.multiple_of(which * (n // 2), 8), n // 2), :]
+
+    y_copies, x_copies, a_copies = [], [], []
+    z_copies = [[] for _ in range(depth.bit_length() - 1)]
+    for i in range(count):
+        off, n = pieces[i]
+        if off >= shard:
+            up_copy.wait_recv()
+        ys_ref[off : off + n, :] = partial(i, 1 - y)
+        copy = remote(ys_ref.at[off : off + n, :], yr_ref.at[off : off + n, :], y_s.at[i], y_r.at[i], across)
+        copy.start()
+        y_copies.append(copy)
+
+    def x_stage(i):
+        off, n = pieces[i]
+        own = partial(i, y)
+        y_copies[i].wait_recv()
+        acc_ref[off : off + n, :] = own + yr_ref[off : off + n, :]
+        h = n // 2
+        short = pl.ds(off // 2, h)
+        copy = remote(acc_ref.at[half(i, 1 - x), :], xrs_ref.at[short, :], x_s.at[i], x_r.at[i], beside)
+        copy.start()
+        x_copies.append(copy)
+
+    def z_stage(i, level):
+        off, n = pieces[i]
+        h = n // 2
+        short = slice(off // 2, off // 2 + h)
+        if level == 0:
+            x_copies[i].wait_recv()
+            total = acc_ref[half(i, x), :] + xrs_ref[short, :]
+        else:
+            z_copies[level - 1][i].wait_recv()
+            total = zs_ref[level - 1, short, :] + zr_ref[level - 1, short, :]
+        if level < len(z_copies):
+            zs_ref[level, short, :] = total
+            bit = 1 << level
+            other = z + bit - 2 * bit * ((z // bit) % 2)
+            copy = remote(zs_ref.at[level, short, :], zr_ref.at[level, short, :], z_s.at[level, i], z_r.at[level, i], along(other))
+            copy.start()
+            z_copies[level].append(copy)
+        else:
+            spot = place(i, x)
+            spot[...] = total * inverse
+            copy = remote(spot, place(i, x), a_s.at[i], a_r.at[i], beside)
+            copy.start()
+            a_copies.append(copy)
+
+    levels = len(z_copies) + 1
+    for t in range(count + levels):
+        if t < count:
+            x_stage(t)
+        for level in range(levels):
+            i = t - 1 - level
+            if 0 <= i < count:
+                z_stage(i, level)
+
+    for copy in a_copies:
+        copy.wait_recv()
+    for d in range(1, depth):
+        pl.when(z + d < depth)(ups[d - 1].wait_send)
+        pl.when(z >= d)(downs[d - 1].wait_send)
+    for copy in core_copies + [swap, low_copy, up_copy] + y_copies + x_copies + sum(z_copies, []) + a_copies:
+        copy.wait_send()
+
+
+def fast(inputs, adapter_down_weight, adapter_up_weight, query, key, value, output_gradient):
+    rows, width = query.shape[1:]
+    model = inputs.shape[2]
+    rank = adapter_down_weight.shape[1]
+    features = adapter_up_weight.shape[0]
+    seq_count = lax.axis_size("seq")
+    dp_count = lax.axis_size("dp")
+    length = rows * seq_count
+    factor = 1.0 / math.sqrt(HEAD_SIZE * length)
+    inverse = 1.0 / math.sqrt(length * dp_count)
+    depth = seq_count // 2
+    stages = depth.bit_length() - 1
+    shard, ushard = model // dp_count, features // dp_count
+    total = shard + ushard
+    count = CHUNKS + 1
+    f32, bf16 = jnp.float32, jnp.bfloat16
+    dma = pltpu.SemaphoreType.DMA
+    vmem = pl.BlockSpec(memory_space=pltpu.VMEM)
+    hbm = pl.BlockSpec(memory_space=pl.ANY)
+    out = pl.pallas_call(
+        functools.partial(fused_kernel, depth, factor, inverse),
+        out_shape=[jax.ShapeDtypeStruct((rows, width), bf16)] * 3
+        + [jax.ShapeDtypeStruct((shard, rank), f32), jax.ShapeDtypeStruct((ushard, rank), f32)],
+        in_specs=[hbm, hbm] + [vmem] * 5,
+        out_specs=[vmem] * 5,
+        scratch_shapes=[
+            pltpu.VMEM((rows, model), bf16),
+            pltpu.VMEM((model, rank), bf16),
+            pltpu.VMEM((2, rows, shard), f32),
+            pltpu.VMEM((2, rows, shard), f32),
+            pltpu.VMEM((2, shard, 2 * rows), bf16),
+            pltpu.VMEM((2, width, width), f32),
+            pltpu.VMEM((depth - 1, width, width), f32),
+            pltpu.VMEM((depth - 1, width, width), f32),
+            pltpu.VMEM((2, width, width), f32),
+            pltpu.VMEM((2, width, width), f32),
+            pltpu.VMEM((rows, rank), f32),
+            pltpu.VMEM((rows, rank), f32),
+            pltpu.VMEM((2, ushard, rank), f32),
+            pltpu.VMEM((2, ushard, rank), f32),
+            pltpu.VMEM((features, rank), f32),
+            pltpu.VMEM((total, rank), f32),
+            pltpu.VMEM((total, rank), f32),
+            pltpu.VMEM((total, rank), f32),
+            pltpu.VMEM((total // 2, rank), f32),
+            pltpu.VMEM((stages, total // 2, rank), f32),
+            pltpu.VMEM((stages, total // 2, rank), f32),
+            dma((2,)), dma((4,)), dma((4,)),
+            dma((depth - 1,)), dma((depth - 1,)), dma((depth - 1,)), dma((depth - 1,)),
+            dma, dma,
+            dma((count,)), dma((count,)), dma((count,)), dma((count,)),
+            dma((stages, count)), dma((stages, count)), dma((count,)), dma((count,)),
+        ],
+        compiler_params=pltpu.CompilerParams(collective_id=0, has_side_effects=True),
+    )(
+        inputs.reshape(rows, model), adapter_down_weight, adapter_up_weight,
+        query.reshape(rows, width), key.reshape(rows, width),
+        value.reshape(rows, width), output_gradient.reshape(rows, width),
+    )
+    return tuple(part.reshape(1, rows, width) for part in out[:3]) + tuple(out[3:])
+
+
 def solution(mesh):
+    fused = fits(mesh.shape["seq"], mesh.shape["dp"])
+    chosen = fast if fused else local
     return jax.shard_map(
-        local,
+        chosen,
         mesh=mesh,
         in_specs=(
             P("dp", "seq", None),

time: 242 us -> 72.5 us (0.30)
  waiting for transfers between devices: 107 us -> 0 us
  blocking collectives: 104 us -> 0 us
  Pallas kernels: 0 us -> 64.5 us
  between operations: 13.9 us -> 0.65 us
  matrix products: 12.6 us -> 0 us
    pallas_call x0 -> x1, Pallas kernels: none -> 64.5 us  [fast(): pl.pallas_call(functools.partial(fused_kernel, depth, factor, inverse), o...]
    all_gather x2 -> x0, blocking collectives: 64.4 us -> none  [entering(): gathered = lax.all_gather(part, axis)]
    reduce_scatter x2 -> x0, waiting for transfers between devices: 63.6 us -> none  [the longest x1 43 us: local(): lax.psum_scatter(lax.dot_general(flattened, low_rank_gradient, contract,...]
    psum x1 -> x0, waiting for transfers between devices: 43 us -> none  [local(): down_grad, up_grad = lax.psum((down_part, up_part), 'seq')]
    psum x1 -> x0, blocking collectives: 39.1 us -> none  [local(): down_grad, up_grad = lax.psum((down_part, up_part), 'seq')]
    dot_general x11 -> x0, matrix products: 12.6 us -> none  [the longest x1 3.12 us: local(): lax.dot_general(gradient_list, low_rank_state, contract, preferred_elemen...]
    unnamed x14 -> x7, local copies, waits for them, and re-layouts: 4.73 us -> 7.02 us
  transfers between devices with their start and end apart: 3 -> 0, of which waited for: 3 -> 0; matrix products, arithmetic and copies ran while one was open for 2% -> 0% of each run, Pallas kernels for 0% -> 0%
where the time goes in v1:
time: 72.5 us; the launch traced here: 72.1 us
  Pallas kernels  64.5 us (89%)
  local copies, waits for them, and re-layouts  7.02 us (10%)
    pallas_call x1, Pallas kernels, fast(): pl.pallas_call(functools.partial(fused_kernel, depth, factor, inverse), o...  64.5 us
    unnamed x7, local copies, waits for them, and re-layouts  7.02 us

profile of v1, /device:TPU:0, one launch (start us, length us, event | category | flops | bytes accessed | tf_op | source)
XLA Modules:
  0.0 72.1 jit_solution(8555404441452012771)
XLA Ops:
  0.6 64.5 %shard_map.110 = (bf16[128,128]{1,0:T(8,128)(2,1)}, bf16[128,128]{1,0:T(8,128)(2,1)}, bf16[128,128]{1,0:T(8,128)(2,1)}, f32[2048,128]{1,0:T(8,128)}, f32[96,128]{1,0:T(8,128)}) custom-call(bf16[128,8192]{1,0:T(8,128)(2,1)} %bitcast.8, bf16[8192,128]{1,0:T(8,128)(2,1)} %w_hbm.1, bf16[384,128]{1,0:T(8,128)(2,1)} %u_ref.1, bf16[128,128]{1,0:T(8,128)(2,1)} %bitcast.9, ...), custom_call_target="tpu_custom_call" | custom-call | tf_op jit(solution)/shard_map/pallas_call | solution.py:368
  65.1 0.0 copy-start
  65.1 1.4 %copy.17 = bf16[1,128,128]{2,1,0:T(8,128)(2,1)} copy(bf16[1,128,128]{2,1,0:T(8,128)(2,1)} %bitcast.15) | data formatting | bytes 65536
  66.5 1.4 %copy.18 = bf16[1,128,128]{2,1,0:T(8,128)(2,1)} copy(bf16[1,128,128]{2,1,0:T(8,128)(2,1)} %bitcast.14) | data formatting | bytes 65536
  67.9 1.4 %copy.19 = bf16[1,128,128]{2,1,0:T(8,128)(2,1)} copy(bf16[1,128,128]{2,1,0:T(8,128)(2,1)} %bitcast.13) | data formatting | bytes 65536
  69.2 2.3 %copy.20 = f32[2048,128]{1,0:T(8,128)} copy(f32[2048,128]{1,0:T(8,128)} %get-tuple-element.23) | data formatting | bytes 2097152
  71.5 0.0 copy-done
  71.5 0.6 copy.21
Async XLA Ops:
  65.1 6.4 %copy-start = (f32[96,128]{1,0:T(8,128)S(1)}, f32[96,128]{1,0:T(8,128)}, u32[]{:S(2)}) copy-start(f32[96,128]{1,0:T(8,128)} %get-tuple-element.24) | copy-start | bytes 147460

commit v2 on v1

--- a/solution.py
+++ b/solution.py
@@ -115,7 +115,8 @@
 
 MESH = pl.DeviceIdType.MESH
 CORES = 2
-CHUNKS = 8
+CHUNKS = 16
+SKEW = 3
 
 
 def fits(seq_count, dp_count):
@@ -132,11 +133,11 @@
     x_hbm, w_hbm, u_ref, q_ref, k_ref, v_ref, g_ref,
     qo_ref, ko_ref, vo_ref, down_ref, up_ref,
     x_ref, w_ref, xs_ref, xr_ref, xt_ref,
-    st_ref, kvr_ref, qgr_ref, sxs_ref, sxr_ref,
+    st_ref, pair_ref, kvr_ref, qgr_ref, ox_ref, sxs_ref, sxr_ref,
     ls_ref, lr_ref, ups_ref, upr_ref, fg_ref,
-    ys_ref, yr_ref, acc_ref, xrs_ref, zs_ref, zr_ref,
+    ys_ref, yr_ref, acc_ref, xrs_ref, zs_ref, zr_ref, us_ref, ur_ref,
     load_sem, core_s, core_r, kv_s, kv_r, qg_s, qg_r, sx_s, sx_r,
-    y_s, y_r, x_s, x_r, z_s, z_r, a_s, a_r,
+    y_s, y_r, x_s, x_r, z_s, z_r, b_s, b_r, a_s, a_r,
 ):
     seq = lax.axis_index("seq")
     dp = lax.axis_index("dp")
@@ -173,13 +174,36 @@
             src_ref=src, dst_ref=dst, send_sem=ssem, recv_sem=rsem, device_id=where, device_id_type=MESH
         )
 
-    ups, downs = [], []
-    for d in range(1, depth):
-        ups.append(remote(st_ref.at[0], kvr_ref.at[d - 1], kv_s.at[d - 1], kv_r.at[d - 1], along(lax.rem(z + d, depth))))
-        downs.append(remote(st_ref.at[1], qgr_ref.at[d - 1], qg_s.at[d - 1], qg_r.at[d - 1], along(lax.rem(z - d + depth, depth))))
-    for d in range(1, depth):
-        pl.when(z + d < depth)(ups[d - 1].start)
-        pl.when(z >= d)(downs[d - 1].start)
+    lead = width // 2
+    first, second = slice(0, lead), slice(lead, width)
+    other = remote(st_ref.at[:, second, :], ox_ref, sx_s.at[1], sx_r.at[1], beside)
+    other.start()
+
+    def scan(source, part, at):
+        ups, downs = [], []
+        for d in range(1, depth):
+            slot = at * (depth - 1) + d - 1
+            ups.append(remote(source.at[0, part, :], kvr_ref.at[d - 1, part, :], kv_s.at[slot], kv_r.at[slot], along(lax.rem(z + d, depth))))
+            downs.append(remote(source.at[1, part, :], qgr_ref.at[d - 1, part, :], qg_s.at[slot], qg_r.at[slot], along(lax.rem(z - d + depth, depth))))
+        for d in range(1, depth):
+            pl.when(z + d < depth)(ups[d - 1].start)
+            pl.when(z >= d)(downs[d - 1].start)
+        return ups, downs
+
+    def collect(ups, downs, part):
+        sxs_ref[:, part, :] = jnp.zeros((2, lead, width), jnp.float32)
+        for d in range(1, depth):
+            @pl.when(z >= d)
+            def _(d=d):
+                ups[d - 1].wait_recv()
+                sxs_ref[0, part, :] += kvr_ref[d - 1, part, :]
+
+            @pl.when(z + d < depth)
+            def _(d=d):
+                downs[d - 1].wait_recv()
+                sxs_ref[1, part, :] += qgr_ref[d - 1, part, :]
+
+    scan_a = scan(st_ref, first, 0)
 
     load_x.wait()
     core_copies = []
@@ -190,6 +214,10 @@
         copy.start()
         core_copies.append(copy)
 
+    other.wait_recv()
+    pair_ref[:, second, :] = st_ref[:, second, :] + ox_ref[...]
+    scan_b = scan(pair_ref, second, 1)
+
     r_idx = lax.broadcasted_iota(jnp.int32, (rows, rows), 0)
     c_idx = lax.broadcasted_iota(jnp.int32, (rows, rows), 1)
     causal = r_idx >= c_idx
@@ -203,30 +231,18 @@
         cols = pl.ds(pl.multiple_of((part * CORES + c) * shard, 128), shard)
         xt_ref[part, :, 0:rows] = x_ref[:, cols].T
 
-    sxs_ref[...] = jnp.zeros_like(sxs_ref)
-    for d in range(1, depth):
-        @pl.when(z >= d)
-        def _(d=d):
-            ups[d - 1].wait_recv()
-            sxs_ref[0] += kvr_ref[d - 1]
-
-        @pl.when(z + d < depth)
-        def _(d=d):
-            downs[d - 1].wait_recv()
-            sxs_ref[1] += qgr_ref[d - 1]
-
-    prefix = sxs_ref[0]
-    suffix = sxs_ref[1]
+    collect(*scan_a, first)
+    lead_sum = sxs_ref[:, first, :]
 
     @pl.when(x == 0)
     def _():
-        sxs_ref[0] += st_ref[0]
+        sxs_ref[0, first, :] += st_ref[0, first, :]
 
     @pl.when(x == 1)
     def _():
-        sxs_ref[1] += st_ref[1]
-
-    swap = remote(sxs_ref, sxr_ref, sx_s, sx_r, beside)
+        sxs_ref[1, first, :] += st_ref[1, first, :]
+
+    swap = remote(sxs_ref.at[:, first, :], sxr_ref, sx_s.at[0], sx_r.at[0], beside)
     swap.start()
 
     load_w.wait()
@@ -235,9 +251,19 @@
         core_copies[part].wait_recv()
         xt_ref[part, :, rows:] = xr_ref[part].astype(jnp.bfloat16).T
 
+    collect(*scan_b, second)
+
+    @pl.when(x == 1)
+    def _():
+        sxs_ref[0, second, :] += ox_ref[0]
+
+    @pl.when(x == 0)
+    def _():
+        sxs_ref[1, second, :] += ox_ref[1]
+
     swap.wait_recv()
-    prefix = (prefix + sxr_ref[0]).astype(jnp.bfloat16)
-    suffix = (suffix + sxr_ref[1]).astype(jnp.bfloat16)
+    states = jnp.concatenate([lead_sum + sxr_ref[...], sxs_ref[:, second, :]], axis=1).astype(jnp.bfloat16)
+    prefix, suffix = states[0], states[1]
     q_grad = (factor * (q_in + dot(g, prefix, 1, 1))).astype(jnp.bfloat16)
     k_grad = (factor * (k_in + dot(v, suffix, 1, 1))).astype(jnp.bfloat16)
     v_grad = (factor * (v_in + dot(k, suffix, 1, 0))).astype(jnp.bfloat16)
@@ -276,14 +302,21 @@
         off, n = pieces[i]
         return pl.ds(pl.multiple_of(off + which * (n // 2), 8), n // 2)
 
-    def place(i, which):
+    def place(i, which, cuts):
         off, n = pieces[i]
-        if off < shard:
-            return down_ref.at[half(i, which), :]
-        return up_ref.at[pl.ds(pl.multiple_of(which * (n // 2), 8), n // 2), :]
+        ref, base = (down_ref, off) if off < shard else (up_ref, 0)
+        return ref.at[pl.ds(pl.multiple_of(base + which * (n // cuts), 8), n // cuts), :]
 
     y_copies, x_copies, a_copies = [], [], []
-    z_copies = [[] for _ in range(depth.bit_length() - 1)]
+    b_copies = []
+    top = depth.bit_length() - 1
+    z_copies = [[] for _ in range(top)]
+    b = z % 2
+
+    def flip(level):
+        bit = 1 << level
+        return z + bit - 2 * bit * ((z // bit) % 2)
+
     for i in range(count):
         off, n = pieces[i]
         if off >= shard:
@@ -306,44 +339,64 @@
 
     def z_stage(i, level):
         off, n = pieces[i]
-        h = n // 2
-        short = slice(off // 2, off // 2 + h)
+        h, e = n // 2, n // 4
         if level == 0:
             x_copies[i].wait_recv()
-            total = acc_ref[half(i, x), :] + xrs_ref[short, :]
+            zs_ref[off // 2 : off // 2 + h, :] = acc_ref[half(i, x), :] + xrs_ref[off // 2 : off // 2 + h, :]
+            away = pl.ds(pl.multiple_of(off // 2 + (1 - b) * e, 8), e)
+            source, target = zs_ref.at[away, :], zr_ref.at[off // 4 : off // 4 + e, :]
+        elif level <= top:
+            z_copies[level - 1][i].wait_recv()
+            short = slice(off // 4, off // 4 + e)
+            if level == 1:
+                kept = zs_ref[pl.ds(pl.multiple_of(off // 2 + b * e, 8), e), :] + zr_ref[short, :]
+            else:
+                kept = us_ref[level - 2, short, :] + ur_ref[level - 2, short, :]
+            if level == top:
+                spot = place(i, x * 2 + b, 4)
+                spot[...] = kept * inverse
+                copy = remote(spot, place(i, x * 2 + b, 4), b_s.at[i], b_r.at[i], along(flip(0)))
+                copy.start()
+                b_copies.append(copy)
+                return
+            us_ref[level - 1, short, :] = kept
+            source, target = us_ref.at[level - 1, short, :], ur_ref.at[level - 1, short, :]
         else:
-            z_copies[level - 1][i].wait_recv()
-            total = zs_ref[level - 1, short, :] + zr_ref[level - 1, short, :]
-        if level < len(z_copies):
-            zs_ref[level, short, :] = total
-            bit = 1 << level
-            other = z + bit - 2 * bit * ((z // bit) % 2)
-            copy = remote(zs_ref.at[level, short, :], zr_ref.at[level, short, :], z_s.at[level, i], z_r.at[level, i], along(other))
-            copy.start()
-            z_copies[level].append(copy)
-        else:
-            spot = place(i, x)
-            spot[...] = total * inverse
-            copy = remote(spot, place(i, x), a_s.at[i], a_r.at[i], beside)
+            b_copies[i].wait_recv()
+            spot = place(i, x, 2)
+            copy = remote(spot, place(i, x, 2), a_s.at[i], a_r.at[i], beside)
             copy.start()
             a_copies.append(copy)
-
-    levels = len(z_copies) + 1
-    for t in range(count + levels):
+            return
+        copy = remote(source, target, z_s.at[level, i], z_r.at[level, i], along(flip(level)))
+        copy.start()
+        z_copies[level].append(copy)
+
+    levels = top + 2
+    for t in range(count + levels * SKEW):
         if t < count:
             x_stage(t)
         for level in range(levels):
-            i = t - 1 - level
+            i = t - SKEW * (1 + level)
             if 0 <= i < count:
                 z_stage(i, level)
 
     for copy in a_copies:
         copy.wait_recv()
-    for d in range(1, depth):
-        pl.when(z + d < depth)(ups[d - 1].wait_send)
-        pl.when(z >= d)(downs[d - 1].wait_send)
-    for copy in core_copies + [swap, low_copy, up_copy] + y_copies + x_copies + sum(z_copies, []) + a_copies:
+    for ups, downs in (scan_a, scan_b):
+        for d in range(1, depth):
+            pl.when(z + d < depth)(ups[d - 1].wait_send)
+            pl.when(z >= d)(downs[d - 1].wait_send)
+    for copy in core_copies + [other, swap, low_copy, up_copy] + y_copies + x_copies + sum(z_copies, []) + b_copies + a_copies:
         copy.wait_send()
+
+
+def write_out(*refs):
+    copies = [pltpu.make_async_copy(refs[i], refs[5 + i], refs[10].at[i]) for i in range(5)]
+    for copy in copies:
+        copy.start()
+    for copy in copies:
+        copy.wait()
 
 
 def fast(inputs, adapter_down_weight, adapter_up_weight, query, key, value, output_gradient):
@@ -365,10 +418,13 @@
     dma = pltpu.SemaphoreType.DMA
     vmem = pl.BlockSpec(memory_space=pltpu.VMEM)
     hbm = pl.BlockSpec(memory_space=pl.ANY)
+    shapes = [jax.ShapeDtypeStruct((rows, width), bf16)] * 3 + [
+        jax.ShapeDtypeStruct((shard, rank), f32),
+        jax.ShapeDtypeStruct((ushard, rank), f32),
+    ]
     out = pl.pallas_call(
         functools.partial(fused_kernel, depth, factor, inverse),
-        out_shape=[jax.ShapeDtypeStruct((rows, width), bf16)] * 3
-        + [jax.ShapeDtypeStruct((shard, rank), f32), jax.ShapeDtypeStruct((ushard, rank), f32)],
+        out_shape=shapes,
         in_specs=[hbm, hbm] + [vmem] * 5,
         out_specs=[vmem] * 5,
         scratch_shapes=[
@@ -378,10 +434,12 @@
             pltpu.VMEM((2, rows, shard), f32),
             pltpu.VMEM((2, shard, 2 * rows), bf16),
             pltpu.VMEM((2, width, width), f32),
+            pltpu.VMEM((2, width, width), f32),
             pltpu.VMEM((depth - 1, width, width), f32),
             pltpu.VMEM((depth - 1, width, width), f32),
+            pltpu.VMEM((2, width // 2, width), f32),
             pltpu.VMEM((2, width, width), f32),
-            pltpu.VMEM((2, width, width), f32),
+            pltpu.VMEM((2, width // 2, width), f32),
             pltpu.VMEM((rows, rank), f32),
             pltpu.VMEM((rows, rank), f32),
             pltpu.VMEM((2, ushard, rank), f32),
@@ -391,20 +449,32 @@
             pltpu.VMEM((total, rank), f32),
             pltpu.VMEM((total, rank), f32),
             pltpu.VMEM((total // 2, rank), f32),
-            pltpu.VMEM((stages, total // 2, rank), f32),
-            pltpu.VMEM((stages, total // 2, rank), f32),
+            pltpu.VMEM((total // 2, rank), f32),
+            pltpu.VMEM((total // 4, rank), f32),
+            pltpu.VMEM((max(stages - 1, 1), total // 4, rank), f32),
+            pltpu.VMEM((max(stages - 1, 1), total // 4, rank), f32),
             dma((2,)), dma((4,)), dma((4,)),
-            dma((depth - 1,)), dma((depth - 1,)), dma((depth - 1,)), dma((depth - 1,)),
-            dma, dma,
+            dma((2 * depth - 2,)), dma((2 * depth - 2,)), dma((2 * depth - 2,)), dma((2 * depth - 2,)),
+            dma((2,)), dma((2,)),
             dma((count,)), dma((count,)), dma((count,)), dma((count,)),
-            dma((stages, count)), dma((stages, count)), dma((count,)), dma((count,)),
+            dma((stages, count)), dma((stages, count)),
+            dma((count,)), dma((count,)), dma((count,)), dma((count,)),
         ],
-        compiler_params=pltpu.CompilerParams(collective_id=0, has_side_effects=True),
+        compiler_params=pltpu.CompilerParams(
+            collective_id=0, has_side_effects=True
+        ),
     )(
         inputs.reshape(rows, model), adapter_down_weight, adapter_up_weight,
         query.reshape(rows, width), key.reshape(rows, width),
         value.reshape(rows, width), output_gradient.reshape(rows, width),
     )
+    out = pl.pallas_call(
+        write_out,
+        out_shape=shapes,
+        in_specs=[vmem] * 5,
+        out_specs=[hbm] * 5,
+        scratch_shapes=[dma((5,))],
+    )(*out)
     return tuple(part.reshape(1, rows, width) for part in out[:3]) + tuple(out[3:])
 
 

time: 72.5 us -> 63 us (0.87)
  local copies, waits for them, and re-layouts: 7.02 us -> 0 us
  Pallas kernels: 64.5 us -> 62.2 us
    unnamed x7 -> x0, local copies, waits for them, and re-layouts: 7.02 us -> none
    pallas_call x1, Pallas kernels: 64.5 us -> 59.9 us  [fast(): pl.pallas_call(functools.partial(fused_kernel, depth, factor, inverse), o...]
    pallas_call x0 -> x1, Pallas kernels: none -> 2.3 us  [fast(): pl.pallas_call(write_out, out_shape=shapes, in_specs=[vmem] * 5, out_spec...]
where the time goes in v2:
time: 63 us; the launch traced here: 62.8 us
  Pallas kernels  62.2 us (99%)
  between operations  0.64 us (1%)
    pallas_call x1, Pallas kernels, fast(): pl.pallas_call(functools.partial(fused_kernel, depth, factor, inverse), o...  59.9 us
    pallas_call x1, Pallas kernels, fast(): pl.pallas_call(write_out, out_shape=shapes, in_specs=[vmem] * 5, out_spec...  2.3 us

profile of v2, /device:TPU:0, one launch (start us, length us, event | category | flops | bytes accessed | tf_op | source)
XLA Modules:
  0.0 62.8 jit_solution(586051081537048737)
XLA Ops:
  0.6 59.9 %shard_map.110 = (bf16[128,128]{1,0:T(8,128)(2,1)}, bf16[128,128]{1,0:T(8,128)(2,1)}, bf16[128,128]{1,0:T(8,128)(2,1)}, f32[2048,128]{1,0:T(8,128)}, f32[96,128]{1,0:T(8,128)}) custom-call(bf16[128,8192]{1,0:T(8,128)(2,1)} %bitcast.8, bf16[8192,128]{1,0:T(8,128)(2,1)} %w_hbm.1, bf16[384,128]{1,0:T(8,128)(2,1)} %u_ref.1, bf16[128,128]{1,0:T(8,128)(2,1)} %bitcast.9, ...), custom_call_target="tpu_custom_call" | custom-call | tf_op jit(solution)/shard_map/pallas_call | solution.py:425
  60.5 2.3 %shard_map.111 = (bf16[128,128]{1,0:T(8,128)(2,1)}, bf16[128,128]{1,0:T(8,128)(2,1)}, bf16[128,128]{1,0:T(8,128)(2,1)}, f32[2048,128]{1,0:T(8,128)}, f32[96,128]{1,0:T(8,128)}) custom-call(bf16[128,128]{1,0:T(8,128)(2,1)} %get-tuple-element.15.refs_0_, bf16[128,128]{1,0:T(8,128)(2,1)} %get-tuple-element.16.refs_1_, ...), custom_call_target="tpu_custom_call" | custom-call | tf_op jit(solution)/shard_map/pallas_call | solution.py:471

commit v3 on v2

--- a/solution.py
+++ b/solution.py
@@ -137,7 +137,7 @@
     ls_ref, lr_ref, ups_ref, upr_ref, fg_ref,
     ys_ref, yr_ref, acc_ref, xrs_ref, zs_ref, zr_ref, us_ref, ur_ref,
     load_sem, core_s, core_r, kv_s, kv_r, qg_s, qg_r, sx_s, sx_r,
-    y_s, y_r, x_s, x_r, z_s, z_r, b_s, b_r, a_s, a_r,
+    y_s, y_r, x_s, x_r, z_s, z_r, b_s, b_r,
 ):
     seq = lax.axis_index("seq")
     dp = lax.axis_index("dp")
@@ -147,6 +147,8 @@
     across = {"seq": seq, "dp": (1 - y) * CORES + c}
     beside = {"seq": z * 2 + (1 - x), "dp": dp}
 
+    corner = {"seq": (z + 1 - 2 * (z % 2)) * 2 + (1 - x), "dp": dp}
+
     def along(other):
         return {"seq": other * 2 + x, "dp": dp}
 
@@ -156,7 +158,7 @@
     load_w.start()
 
     barrier = pltpu.get_barrier_semaphore()
-    friends = [mate, across, beside] + [along(lax.rem(z + d, depth)) for d in range(1, depth)]
+    friends = [mate, across, beside, corner] + [along(lax.rem(z + d, depth)) for d in range(1, depth)]
     for friend in friends:
         pl.semaphore_signal(barrier, inc=1, device_id=friend, device_id_type=MESH)
 
@@ -245,8 +247,6 @@
     swap = remote(sxs_ref.at[:, first, :], sxr_ref, sx_s.at[0], sx_r.at[0], beside)
     swap.start()
 
-    load_w.wait()
-    low = jnp.dot(x_ref[...], w_ref[...], preferred_element_type=jnp.float32).astype(jnp.bfloat16)
     for part in range(2):
         core_copies[part].wait_recv()
         xt_ref[part, :, rows:] = xr_ref[part].astype(jnp.bfloat16).T
@@ -276,6 +276,50 @@
     ko_ref[...] = k_grad
     vo_ref[...] = v_grad
 
+    low_copy.wait_recv()
+    both = jnp.concatenate([low_grad, lr_ref[...].astype(jnp.bfloat16)], axis=0)
+
+    size = shard // CHUNKS
+    pieces = [(i * size, size) for i in range(CHUNKS)] + [(shard, ushard)]
+    count = len(pieces)
+
+    def partial(i, part):
+        off, n = pieces[i]
+        if off < shard:
+            return jnp.dot(xt_ref[part, off : off + n, :], both, preferred_element_type=jnp.float32)
+        mine = pl.ds(pl.multiple_of((part * CORES + c) * ushard, 8), ushard)
+        return fg_ref[mine, :] + upr_ref[part]
+
+    def half(i, which):
+        off, n = pieces[i]
+        return pl.ds(pl.multiple_of(off + which * (n // 2), 8), n // 2)
+
+    def place(i, which, cuts):
+        off, n = pieces[i]
+        ref, base = (down_ref, off) if off < shard else (up_ref, 0)
+        return ref.at[pl.ds(pl.multiple_of(base + which * (n // cuts), 8), n // cuts), :]
+
+    y_copies, x_copies = [], []
+    b_copies = []
+    top = depth.bit_length() - 1
+    z_copies = [[] for _ in range(top)]
+    b = z % 2
+
+    def flip(level):
+        bit = 1 << level
+        return z + bit - 2 * bit * ((z // bit) % 2)
+
+    def y_stage(i):
+        off, n = pieces[i]
+        ys_ref[off : off + n, :] = partial(i, 1 - y)
+        copy = remote(ys_ref.at[off : off + n, :], yr_ref.at[off : off + n, :], y_s.at[i], y_r.at[i], across)
+        copy.start()
+        y_copies.append(copy)
+
+    for i in range(count - 1):
+        y_stage(i)
+    load_w.wait()
+    low = jnp.dot(x_ref[...], w_ref[...], preferred_element_type=jnp.float32).astype(jnp.bfloat16)
     up_all = dot(fg, low, 0, 0)
     fg_ref[...] = up_all
     for part in range(2):
@@ -284,47 +328,8 @@
     up_copy = remote(ups_ref, upr_ref, core_s.at[3], core_r.at[3], mate)
     up_copy.start()
 
-    low_copy.wait_recv()
-    both = jnp.concatenate([low_grad, lr_ref[...].astype(jnp.bfloat16)], axis=0)
-
-    size = shard // CHUNKS
-    pieces = [(i * size, size) for i in range(CHUNKS)] + [(shard, ushard)]
-    count = len(pieces)
-
-    def partial(i, part):
-        off, n = pieces[i]
-        if off < shard:
-            return jnp.dot(xt_ref[part, off : off + n, :], both, preferred_element_type=jnp.float32)
-        mine = pl.ds(pl.multiple_of((part * CORES + c) * ushard, 8), ushard)
-        return fg_ref[mine, :] + upr_ref[part]
-
-    def half(i, which):
-        off, n = pieces[i]
-        return pl.ds(pl.multiple_of(off + which * (n // 2), 8), n // 2)
-
-    def place(i, which, cuts):
-        off, n = pieces[i]
-        ref, base = (down_ref, off) if off < shard else (up_ref, 0)
-        return ref.at[pl.ds(pl.multiple_of(base + which * (n // cuts), 8), n // cuts), :]
-
-    y_copies, x_copies, a_copies = [], [], []
-    b_copies = []
-    top = depth.bit_length() - 1
-    z_copies = [[] for _ in range(top)]
-    b = z % 2
-
-    def flip(level):
-        bit = 1 << level
-        return z + bit - 2 * bit * ((z // bit) % 2)
-
-    for i in range(count):
-        off, n = pieces[i]
-        if off >= shard:
-            up_copy.wait_recv()
-        ys_ref[off : off + n, :] = partial(i, 1 - y)
-        copy = remote(ys_ref.at[off : off + n, :], yr_ref.at[off : off + n, :], y_s.at[i], y_r.at[i], across)
-        copy.start()
-        y_copies.append(copy)
+    up_copy.wait_recv()
+    y_stage(count - 1)
 
     def x_stage(i):
         off, n = pieces[i]
@@ -345,7 +350,7 @@
             zs_ref[off // 2 : off // 2 + h, :] = acc_ref[half(i, x), :] + xrs_ref[off // 2 : off // 2 + h, :]
             away = pl.ds(pl.multiple_of(off // 2 + (1 - b) * e, 8), e)
             source, target = zs_ref.at[away, :], zr_ref.at[off // 4 : off // 4 + e, :]
-        elif level <= top:
+        else:
             z_copies[level - 1][i].wait_recv()
             short = slice(off // 4, off // 4 + e)
             if level == 1:
@@ -355,24 +360,18 @@
             if level == top:
                 spot = place(i, x * 2 + b, 4)
                 spot[...] = kept * inverse
-                copy = remote(spot, place(i, x * 2 + b, 4), b_s.at[i], b_r.at[i], along(flip(0)))
-                copy.start()
-                b_copies.append(copy)
+                for at, where in enumerate((beside, along(flip(0)), corner)):
+                    copy = remote(spot, place(i, x * 2 + b, 4), b_s.at[at, i], b_r.at[at, i], where)
+                    copy.start()
+                    b_copies.append(copy)
                 return
             us_ref[level - 1, short, :] = kept
             source, target = us_ref.at[level - 1, short, :], ur_ref.at[level - 1, short, :]
-        else:
-            b_copies[i].wait_recv()
-            spot = place(i, x, 2)
-            copy = remote(spot, place(i, x, 2), a_s.at[i], a_r.at[i], beside)
-            copy.start()
-            a_copies.append(copy)
-            return
         copy = remote(source, target, z_s.at[level, i], z_r.at[level, i], along(flip(level)))
         copy.start()
         z_copies[level].append(copy)
 
-    levels = top + 2
+    levels = top + 1
     for t in range(count + levels * SKEW):
         if t < count:
             x_stage(t)
@@ -381,13 +380,13 @@
             if 0 <= i < count:
                 z_stage(i, level)
 
-    for copy in a_copies:
+    for copy in b_copies:
         copy.wait_recv()
     for ups, downs in (scan_a, scan_b):
         for d in range(1, depth):
             pl.when(z + d < depth)(ups[d - 1].wait_send)
             pl.when(z >= d)(downs[d - 1].wait_send)
-    for copy in core_copies + [other, swap, low_copy, up_copy] + y_copies + x_copies + sum(z_copies, []) + b_copies + a_copies:
+    for copy in core_copies + [other, swap, low_copy, up_copy] + y_copies + x_copies + sum(z_copies, []) + b_copies:
         copy.wait_send()
 
 
@@ -458,7 +457,7 @@
             dma((2,)), dma((2,)),
             dma((count,)), dma((count,)), dma((count,)), dma((count,)),
             dma((stages, count)), dma((stages, count)),
-            dma((count,)), dma((count,)), dma((count,)), dma((count,)),
+            dma((3, count)), dma((3, count)),
         ],
         compiler_params=pltpu.CompilerParams(
             collective_id=0, has_side_effects=True

time: 63 us -> 62.7 us (level)
  no operation moved by 1% of the time
where the time goes in v3:
time: 62.7 us; the launch traced here: 62.5 us
  Pallas kernels  61.8 us (99%)
  between operations  0.64 us (1%)
    pallas_call x1, Pallas kernels, fast(): pl.pallas_call(functools.partial(fused_kernel, depth, factor, inverse), o...  59.5 us
    pallas_call x1, Pallas kernels, fast(): pl.pallas_call(write_out, out_shape=shapes, in_specs=[vmem] * 5, out_spec...  2.3 us

profile of v3, /device:TPU:0, one launch (start us, length us, event | category | flops | bytes accessed | tf_op | source)
XLA Modules:
  0.0 62.5 jit_solution(12820893498334411331)
XLA Ops:
  0.6 59.5 %shard_map.110 = (bf16[128,128]{1,0:T(8,128)(2,1)}, bf16[128,128]{1,0:T(8,128)(2,1)}, bf16[128,128]{1,0:T(8,128)(2,1)}, f32[2048,128]{1,0:T(8,128)}, f32[96,128]{1,0:T(8,128)}) custom-call(bf16[128,8192]{1,0:T(8,128)(2,1)} %bitcast.8, bf16[8192,128]{1,0:T(8,128)(2,1)} %w_hbm.1, bf16[384,128]{1,0:T(8,128)(2,1)} %u_ref.1, bf16[128,128]{1,0:T(8,128)(2,1)} %bitcast.9, ...), custom_call_target="tpu_custom_call" | custom-call | tf_op jit(solution)/shard_map/pallas_call | solution.py:424
  60.2 2.3 %shard_map.111 = (bf16[128,128]{1,0:T(8,128)(2,1)}, bf16[128,128]{1,0:T(8,128)(2,1)}, bf16[128,128]{1,0:T(8,128)(2,1)}, f32[2048,128]{1,0:T(8,128)}, f32[96,128]{1,0:T(8,128)}) custom-call(bf16[128,128]{1,0:T(8,128)(2,1)} %get-tuple-element.15.refs_0_, bf16[128,128]{1,0:T(8,128)(2,1)} %get-tuple-element.16.refs_1_, ...), custom_call_target="tpu_custom_call" | custom-call | tf_op jit(solution)/shard_map/pallas_call | solution.py:470

commit v4 on v2

--- a/solution.py
+++ b/solution.py
@@ -245,8 +245,6 @@
     swap = remote(sxs_ref.at[:, first, :], sxr_ref, sx_s.at[0], sx_r.at[0], beside)
     swap.start()
 
-    load_w.wait()
-    low = jnp.dot(x_ref[...], w_ref[...], preferred_element_type=jnp.float32).astype(jnp.bfloat16)
     for part in range(2):
         core_copies[part].wait_recv()
         xt_ref[part, :, rows:] = xr_ref[part].astype(jnp.bfloat16).T
@@ -276,6 +274,50 @@
     ko_ref[...] = k_grad
     vo_ref[...] = v_grad
 
+    low_copy.wait_recv()
+    both = jnp.concatenate([low_grad, lr_ref[...].astype(jnp.bfloat16)], axis=0)
+
+    size = shard // CHUNKS
+    pieces = [(i * size, size) for i in range(CHUNKS)] + [(shard, ushard)]
+    count = len(pieces)
+
+    def partial(i, part):
+        off, n = pieces[i]
+        if off < shard:
+            return jnp.dot(xt_ref[part, off : off + n, :], both, preferred_element_type=jnp.float32)
+        mine = pl.ds(pl.multiple_of((part * CORES + c) * ushard, 8), ushard)
+        return fg_ref[mine, :] + upr_ref[part]
+
+    def half(i, which):
+        off, n = pieces[i]
+        return pl.ds(pl.multiple_of(off + which * (n // 2), 8), n // 2)
+
+    def place(i, which, cuts):
+        off, n = pieces[i]
+        ref, base = (down_ref, off) if off < shard else (up_ref, 0)
+        return ref.at[pl.ds(pl.multiple_of(base + which * (n // cuts), 8), n // cuts), :]
+
+    y_copies, x_copies, a_copies = [], [], []
+    b_copies = []
+    top = depth.bit_length() - 1
+    z_copies = [[] for _ in range(top)]
+    b = z % 2
+
+    def flip(level):
+        bit = 1 << level
+        return z + bit - 2 * bit * ((z // bit) % 2)
+
+    def y_stage(i):
+        off, n = pieces[i]
+        ys_ref[off : off + n, :] = partial(i, 1 - y)
+        copy = remote(ys_ref.at[off : off + n, :], yr_ref.at[off : off + n, :], y_s.at[i], y_r.at[i], across)
+        copy.start()
+        y_copies.append(copy)
+
+    for i in range(count - 1):
+        y_stage(i)
+    load_w.wait()
+    low = jnp.dot(x_ref[...], w_ref[...], preferred_element_type=jnp.float32).astype(jnp.bfloat16)
     up_all = dot(fg, low, 0, 0)
     fg_ref[...] = up_all
     for part in range(2):
@@ -284,47 +326,8 @@
     up_copy = remote(ups_ref, upr_ref, core_s.at[3], core_r.at[3], mate)
     up_copy.start()
 
-    low_copy.wait_recv()
-    both = jnp.concatenate([low_grad, lr_ref[...].astype(jnp.bfloat16)], axis=0)
-
-    size = shard // CHUNKS
-    pieces = [(i * size, size) for i in range(CHUNKS)] + [(shard, ushard)]
-    count = len(pieces)
-
-    def partial(i, part):
-        off, n = pieces[i]
-        if off < shard:
-            return jnp.dot(xt_ref[part, off : off + n, :], both, preferred_element_type=jnp.float32)
-        mine = pl.ds(pl.multiple_of((part * CORES + c) * ushard, 8), ushard)
-        return fg_ref[mine, :] + upr_ref[part]
-
-    def half(i, which):
-        off, n = pieces[i]
-        return pl.ds(pl.multiple_of(off + which * (n // 2), 8), n // 2)
-
-    def place(i, which, cuts):
-        off, n = pieces[i]
-        ref, base = (down_ref, off) if off < shard else (up_ref, 0)
-        return ref.at[pl.ds(pl.multiple_of(base + which * (n // cuts), 8), n // cuts), :]
-
-    y_copies, x_copies, a_copies = [], [], []
-    b_copies = []
-    top = depth.bit_length() - 1
-    z_copies = [[] for _ in range(top)]
-    b = z % 2
-
-    def flip(level):
-        bit = 1 << level
-        return z + bit - 2 * bit * ((z // bit) % 2)
-
-    for i in range(count):
-        off, n = pieces[i]
-        if off >= shard:
-            up_copy.wait_recv()
-        ys_ref[off : off + n, :] = partial(i, 1 - y)
-        copy = remote(ys_ref.at[off : off + n, :], yr_ref.at[off : off + n, :], y_s.at[i], y_r.at[i], across)
-        copy.start()
-        y_copies.append(copy)
+    up_copy.wait_recv()
+    y_stage(count - 1)
 
     def x_stage(i):
         off, n = pieces[i]

time: 63 us -> 62.7 us (level)
  no operation moved by 1% of the time
where the time goes in v4:
time: 62.7 us; the launch traced here: 62.6 us
  Pallas kernels  61.9 us (99%)
  between operations  0.64 us (1%)
    pallas_call x1, Pallas kernels, fast(): pl.pallas_call(functools.partial(fused_kernel, depth, factor, inverse), o...  59.6 us
    pallas_call x1, Pallas kernels, fast(): pl.pallas_call(write_out, out_shape=shapes, in_specs=[vmem] * 5, out_spec...  2.3 us

profile of v4, /device:TPU:0, one launch (start us, length us, event | category | flops | bytes accessed | tf_op | source)
XLA Modules:
  0.0 62.6 jit_solution(10316283171902748201)
XLA Ops:
  0.6 59.6 %shard_map.110 = (bf16[128,128]{1,0:T(8,128)(2,1)}, bf16[128,128]{1,0:T(8,128)(2,1)}, bf16[128,128]{1,0:T(8,128)(2,1)}, f32[2048,128]{1,0:T(8,128)}, f32[96,128]{1,0:T(8,128)}) custom-call(bf16[128,8192]{1,0:T(8,128)(2,1)} %bitcast.8, bf16[8192,128]{1,0:T(8,128)(2,1)} %w_hbm.1, bf16[384,128]{1,0:T(8,128)(2,1)} %u_ref.1, bf16[128,128]{1,0:T(8,128)(2,1)} %bitcast.9, ...), custom_call_target="tpu_custom_call" | custom-call | tf_op jit(solution)/shard_map/pallas_call | solution.py:428
  60.3 2.3 %shard_map.111 = (bf16[128,128]{1,0:T(8,128)(2,1)}, bf16[128,128]{1,0:T(8,128)(2,1)}, bf16[128,128]{1,0:T(8,128)(2,1)}, f32[2048,128]{1,0:T(8,128)}, f32[96,128]{1,0:T(8,128)}) custom-call(bf16[128,128]{1,0:T(8,128)(2,1)} %get-tuple-element.15.refs_0_, bf16[128,128]{1,0:T(8,128)(2,1)} %get-tuple-element.16.refs_1_, ...), custom_call_target="tpu_custom_call" | custom-call | tf_op jit(solution)/shard_map/pallas_call | solution.py:474
